TPU v7x, 32 devices: a whole 2x2x4 slice. The times are simulated.
32 devices in a mesh: blk: 16 (over z, y, x), feat: 2 (over core).
Axes of the slice: x: 2, y: 2, z: 4, core: 2. Of those that a mesh axis runs over, the one named last changes fastest.
Arguments:
- points: bfloat16 [16384, 64], P('blk', 'feat'), may hold values from -1.5 to 1.5
- vectors: bfloat16 [16384, 64], P('blk', 'feat'), may hold values from -5.5 to 5.5
- lengthscale: float32 [64], replicated, may hold values from 0.5 to 2
- outscale: float32 [1], replicated, may hold values from 0.1 to 0.4
- noise: float32 [1], replicated, may hold values from 0.05 to 0.5
Outputs:
- product: float32 [16384, 64], P('blk', 'feat')
All inputs are finite; a program needn't handle non-finite values.
Results may differ from a plain program's by a relative error of at most 0.0026.
Values may be sent and summed in bfloat16 or wider, within the bound.
A program may use at most 64 MiB of HBM per device.

v0:
```python
import math

import jax
import jax.numpy as jnp
from jax import lax
from jax.sharding import PartitionSpec as P


def squares(values):
    wide = values.astype(jnp.float32)
    return jnp.sum(wide * wide, axis=1)


def kernel_tile(rows_left, norms_left, rows_right, norms_right, amplitude):
    inner = lax.dot_general(
        rows_left, rows_right, (((1,), (1,)), ((), ())), preferred_element_type=jnp.float32
    )
    distance = jnp.maximum(norms_left[:, None] + norms_right[None, :] - 2.0 * inner, 0.0)
    return (amplitude * jnp.exp(-0.5 * distance)).astype(jnp.bfloat16)


def per_device(points, vectors, lengthscale, outscale, noise):
    feature_width = points.shape[1]
    feat_index = lax.axis_index("feat")
    length_slice = lax.dynamic_slice_in_dim(lengthscale, feat_index * feature_width, feature_width)
    scaled = (points.astype(jnp.float32) / length_slice).astype(jnp.bfloat16)
    whole_points, whole_vectors = (
        lax.all_gather(scaled, "feat", axis=1, tiled=True),
        lax.all_gather(vectors, "feat", axis=1, tiled=True),
    )
    block_rows = points.shape[0]
    row_share = block_rows // lax.axis_size("feat")
    amplitude = outscale[0]
    vector_count = whole_vectors.shape[1]
    whole_norms = squares(whole_points)
    share_points = lax.dynamic_slice_in_dim(whole_points, feat_index * row_share, row_share, 0)
    share_vectors = lax.dynamic_slice_in_dim(whole_vectors, feat_index * row_share, row_share, 0)
    guest_points, guest_vectors = (
        lax.all_gather(share_points, "blk", axis=0, tiled=True),
        lax.all_gather(share_vectors, "blk", axis=0, tiled=True),
    )
    guest_total = guest_points.shape[0]
    step_rows = math.gcd(guest_total, 2048)
    step_count = guest_total // step_rows
    point_groups = guest_points.reshape(step_count, step_rows, guest_points.shape[1])
    vector_groups = guest_vectors.reshape(step_count, step_rows, guest_vectors.shape[1])

    def advance(partial_value, paired):
        group_points, group_vectors = paired
        kernel_block = kernel_tile(
            whole_points, whole_norms, group_points, squares(group_points), amplitude
        )
        return (
            partial_value
            + jnp.dot(kernel_block, group_vectors, preferred_element_type=jnp.float32),
            None,
        )

    start_sum = jnp.zeros((block_rows, vector_count), jnp.float32)
    direct, unused = lax.scan(advance, start_sum, (point_groups, vector_groups))
    result = lax.psum_scatter(direct, "feat", scatter_dimension=1, tiled=True)
    return result + noise[0] * vectors.astype(jnp.float32)


def solution(mesh):
    placed = (P("blk", "feat"), P("blk", "feat"), P(), P(), P())
    return jax.shard_map(
        per_device, mesh=mesh, in_specs=placed, out_specs=P("blk", "feat"), check_vma=False
    )
```

profile of v0, /device:TPU:0, one launch (start us, length us, event | category | flops | bytes accessed | tf_op | source)
XLA Modules:
  0.0 162.1 jit_solution(330200203575874571)
XLA Ops:
  6.5 0.0 all-gather.3.cloned.1.call-start
  6.5 0.7 dynamic_slice.16
  7.3 0.9 divide_convert_fusion
  8.2 2.0 %all_gather.12 = bf16[1024,64]{0,1:T(8,128)(2,1)S(1)} all-gather(bf16[1024,32]{0,1:T(8,128)(2,1)S(1)} %divide_convert_fusion), channel_id=1, replica_groups=mesh['blk'=16,'feat'=2] {'feat'}, dimensions={1}, use_global_device_ids=true | all-gather | bytes 196608 | tf_op jit(solution)/shard_map/all_gather | solution.py:28
  10.2 0.6 constant_dynamic-slice_fusion.1
  10.9 0.0 all-gather.3.cloned.1.call-update
  10.9 0.0 all-gather.5.cloned.1.call-start
  10.9 2.1 %all_gather.14 = bf16[1024,64]{0,1:T(8,128)(2,1)S(1)} all-gather(bf16[1024,32]{0,1:T(8,128)(2,1)} %param.8), channel_id=1, replica_groups=mesh['blk'=16,'feat'=2] {'feat'}, dimensions={1}, use_global_device_ids=true | all-gather | bytes 196608 | tf_op jit(solution)/shard_map/all_gather | solution.py:29
  13.0 0.6 constant_dynamic-slice_fusion
  13.7 0.0 all-gather.5.cloned.1.call-update
  13.7 0.0 reduce-scatter.2.cloned.1.call-start
  13.7 0.2 copy.10
  14.0 52.8 %all-gather.3.cloned.1.call-done = bf16[8192,64]{0,1:T(8,128)(2,1)} async-done(((bf16[512,64]{0,1:T(8,128)(2,1)}), bf16[8192,64]{0,1:T(8,128)(2,1)}) %all-gather.3.cloned.1.call-update) | async-done | bytes 1048592 | tf_op jit(solution)/shard_map/all_gather | solution.py:39
  66.8 2.0 %copy.11 = bf16[8192,64]{1,0:T(8,128)(2,1)S(1)} copy(bf16[8192,64]{0,1:T(8,128)(2,1)} %all-gather.3.cloned.1.call-done) | data formatting | bytes 2097152
  68.8 53.2 %all-gather.5.cloned.1.call-done = bf16[8192,64]{0,1:T(8,128)(2,1)} async-done(((bf16[512,64]{0,1:T(8,128)(2,1)}), bf16[8192,64]{0,1:T(8,128)(2,1)}) %all-gather.5.cloned.1.call-update) | async-done | bytes 1048592 | tf_op jit(solution)/shard_map/all_gather | solution.py:40
  122.0 2.8 %copy.8 = bf16[8192,64]{1,0:T(8,128)(2,1)} copy(bf16[8192,64]{0,1:T(8,128)(2,1)} %all-gather.5.cloned.1.call-done) | data formatting | bytes 2097152 | tf_op jit(solution)/shard_map/all_gather | solution.py:40
  124.7 0.0 copy-start
  124.7 21.3 %while.11 = (s32[]{:T(128)}, f32[1024,64]{0,1:T(8,128)S(1)}, f32[]{:T(128)}, f32[1024]{0:T(1024)S(1)}, bf16[4,2048,64]{2,1,0:T(8,128)(2,1)S(1)}, /*index=5*/bf16...) while((s32[]{:T(128)}, f32[1024,64]{0,1:T(8,128)S(1)}, f32[]{:T(128)}, ...), condition=%wide.region_3.4_spmd.clone, body=%wide.region_1.3_spmd.clone.sunk | while | flops 552073216 | bytes 2119275 | solution.py:60
  124.7 0.3 multiply_reduce_fusion.3
  125.1 5.0 %fusion.26 = f32[1024,64]{0,1:T(8,128)S(1)} fusion(bf16[1024,64]{1,0:T(8,128)(2,1)S(1)} %get-tuple-element.154, f32[2048]{0:T(1024)S(1)} %multiply_reduce_fusion.3, f32[1024]{0:T(1024)S(1)} %get-tuple-element.152, f32[]{:T(128)} %get-tuple-element.151, bf16[4,2048,64]{2,1,0:T(8,128)(2,1)} %get-tuple-element.155, s32[]{:T(128)} %get-tuple-element.140, ...), kind=kOutput, calls=%fused_computation.7.clone.1 | convolution fusion | flops 551682048 | bytes 1848833 | tf_op jit(solution)/shard_map/while/body/eval_jaxpr/dot_general | solution.py:55
  130.1 0.3 multiply_reduce_fusion.3
  130.4 5.0 %fusion.26 = f32[1024,64]{0,1:T(8,128)S(1)} fusion(bf16[1024,64]{1,0:T(8,128)(2,1)S(1)} %get-tuple-element.154, f32[2048]{0:T(1024)S(1)} %multiply_reduce_fusion.3, f32[1024]{0:T(1024)S(1)} %get-tuple-element.152, f32[]{:T(128)} %get-tuple-element.151, bf16[4,2048,64]{2,1,0:T(8,128)(2,1)} %get-tuple-element.155, s32[]{:T(128)} %get-tuple-element.140, ...), kind=kOutput, calls=%fused_computation.7.clone.1 | convolution fusion | flops 551682048 | bytes 1848833 | tf_op jit(solution)/shard_map/while/body/eval_jaxpr/dot_general | solution.py:55
  135.4 0.3 multiply_reduce_fusion.3
  135.8 5.0 %fusion.26 = f32[1024,64]{0,1:T(8,128)S(1)} fusion(bf16[1024,64]{1,0:T(8,128)(2,1)S(1)} %get-tuple-element.154, f32[2048]{0:T(1024)S(1)} %multiply_reduce_fusion.3, f32[1024]{0:T(1024)S(1)} %get-tuple-element.152, f32[]{:T(128)} %get-tuple-element.151, bf16[4,2048,64]{2,1,0:T(8,128)(2,1)} %get-tuple-element.155, s32[]{:T(128)} %get-tuple-element.140, ...), kind=kOutput, calls=%fused_computation.7.clone.1 | convolution fusion | flops 551682048 | bytes 1848833 | tf_op jit(solution)/shard_map/while/body/eval_jaxpr/dot_general | solution.py:55
  140.8 0.3 multiply_reduce_fusion.3
  141.1 5.0 %fusion.26 = f32[1024,64]{0,1:T(8,128)S(1)} fusion(bf16[1024,64]{1,0:T(8,128)(2,1)S(1)} %get-tuple-element.154, f32[2048]{0:T(1024)S(1)} %multiply_reduce_fusion.3, f32[1024]{0:T(1024)S(1)} %get-tuple-element.152, f32[]{:T(128)} %get-tuple-element.151, bf16[4,2048,64]{2,1,0:T(8,128)(2,1)} %get-tuple-element.155, s32[]{:T(128)} %get-tuple-element.140, ...), kind=kOutput, calls=%fused_computation.7.clone.1 | convolution fusion | flops 551682048 | bytes 1848833 | tf_op jit(solution)/shard_map/while/body/eval_jaxpr/dot_general | solution.py:55
  146.1 0.0 copy-start.1
  146.1 0.7 copy-done.1
  146.8 0.0 reduce-scatter.2.cloned.1.call-update
  147.5 6.6 %reduce-scatter.2.cloned.1.call-done = f32[1024,32]{0,1:T(8,128)} async-done(((f32[1024,64]{0,1:T(8,128)}), f32[1024,32]{0,1:T(8,128)}) %reduce-scatter.2.cloned.1.call-update) | async-done | bytes 131088 | tf_op jit(solution)/shard_map/reduce_scatter | solution.py:61
  154.0 0.0 copy-done
  154.0 1.6 multiply_add_fusion
  (2 shorter events, 0.0 us)
Async XLA Ops:
  6.5 60.2 %all-gather.3.cloned.1.call-start = ((), (), s32[]{:S(2)}) async-start(), calls=%async_computation.1 | async-start | bytes 1114112 | tf_op jit(solution)/shard_map/all_gather | solution.py:39
  10.9 111.1 %all-gather.5.cloned.1.call-start = ((), (), s32[]{:S(2)}) async-start(), calls=%async_computation.2 | async-start | bytes 1114112 | tf_op jit(solution)/shard_map/all_gather | solution.py:40
  13.7 140.3 %reduce-scatter.2.cloned.1.call-start = ((), (), s32[]{:S(2)}) async-start(), calls=%async_computation.3 | async-start | bytes 393216 | tf_op jit(solution)/shard_map/reduce_scatter | solution.py:61
  124.7 29.3 %copy-start = (bf16[1024,32]{0,1:T(8,128)(2,1)S(1)}, bf16[1024,32]{0,1:T(8,128)(2,1)}, u32[]{:S(2)}) copy-start(bf16[1024,32]{0,1:T(8,128)(2,1)} %param.8) | copy-start | bytes 196612
  146.1 0.7 copy-start.1
Sparse Core Ops, SparseCore 0:
  11.0 55.7 all-gather.2
  69.5 52.4 all-gather.4
  146.9 7.0 reduce-scatter.1
where the time goes:
time: 163 us; the launch traced here: 162 us
  waiting for transfers between devices  113 us (69%)
  matrix products  19.8 us (12%)
  between operations  13.8 us (8%)
  local copies, waits for them, and re-layouts  7.62 us (5%)
  blocking collectives  4.15 us (3%)
  other arithmetic  3.93 us (2%)
    all_gather x1, waiting for transfers between devices, per_device(): lax.all_gather(share_vectors, 'blk', axis=0, tiled=True)  53.2 us
    all_gather x1, waiting for transfers between devices, per_device(): lax.all_gather(share_points, 'blk', axis=0, tiled=True)  52.8 us
    dot_general x4, matrix products, advance(): jnp.dot(kernel_block, group_vectors, preferred_element_type=jnp.float32)  19.8 us
    reduce_scatter x1, waiting for transfers between devices, per_device(): result = lax.psum_scatter(direct, 'feat', scatter_dimension=1, tiled=True)  6.58 us
  transfers between devices with their start and end apart: 3, of which 3 were waited for; matrix products, arithmetic and copies ran while one was open for 2% of the time, Pallas kernels for 0%

commit v1 on v0

v1 whole, which is shorter than its diff:
```python
import functools

import jax
import jax.numpy as jnp
from jax import lax
from jax.experimental import pallas as pl
from jax.experimental.pallas import tpu as pltpu
from jax.sharding import PartitionSpec as P

LOG2E = 1.4426950408889634
F32 = jnp.float32
BF16 = jnp.bfloat16
EXTRA = 16


def pieces(value):
    first = value.astype(BF16).astype(F32)
    rest = value - first
    second = rest.astype(BF16).astype(F32)
    return first, second, rest - second


def extra_rows(rows):
    shape = (EXTRA, rows[0].shape[1])
    place = lax.broadcasted_iota(jnp.int32, shape, 0)
    out = jnp.zeros(shape, F32)
    for index, row in enumerate(rows):
        out = jnp.where(place == index, row, out)
    return out.astype(BF16)


def visit_order(line, inner):
    if inner == 1:
        return [(rank, 0, 0) for rank in range(line)]
    near = [(rank, b, 0) for rank in range(line) for b in range(2)]
    order = []
    sent = 0
    for place, item in enumerate(near):
        order.append(item)
        if place >= 2:
            order.append((near[sent][0], near[sent][1], 1))
            sent += 1
    order += [(near[i][0], near[i][1], 1) for i in range(sent, len(near))]
    return order


def pick(step, values):
    out = jnp.int32(values[0])
    for index, value in enumerate(values):
        if value != values[0]:
            out = jnp.where(step == index, jnp.int32(value), out)
    return out


def kernel(
    line, inner, points, vectors, lengths, outscale, noise, result,
    blocks, own, own_wide, total, inbox, mine,
    local_sem, pair_send, pair_recv, line_send, b_send, c_send, recv, part_send, part_recv,
):
    me = lax.axis_index("blk")
    core = lax.axis_index("feat")
    other = 1 - core
    half, rows = points.shape
    feats = own.shape[0]
    share = rows // 2
    z = me // (inner * inner)
    stride_b = jnp.where(core == 0, inner, 1)
    stride_c = jnp.where(core == 0, 1, inner)
    low = me % inner
    high = (me // inner) % inner
    bit_b = jnp.where(core == 0, high, low)
    bit_c = jnp.where(core == 0, low, high)
    peer_b = me + stride_b * (1 - 2 * bit_b)
    peer_c = me + stride_c * (1 - 2 * bit_c)
    step_z = inner * inner
    has_up = z < line - 1
    has_down = z > 0

    def place_of(blk, feat):
        return {"blk": blk, "feat": feat}

    def remote(src, dst, send, arrive, blk, feat):
        return pltpu.make_async_remote_copy(
            src_ref=src, dst_ref=dst, send_sem=send, recv_sem=arrive,
            device_id=place_of(blk, feat), device_id_type=pl.DeviceIdType.MESH,
        )

    barrier = pltpu.get_barrier_semaphore()

    def greet(blk, feat):
        pl.semaphore_signal(
            barrier, inc=1, device_id=place_of(blk, feat), device_id_type=pl.DeviceIdType.MESH
        )

    greet(me, other)
    if inner == 2:
        greet(peer_b, core)
        greet(peer_c, core)

    @pl.when(has_up)
    def _():
        greet(me + step_z, core)

    @pl.when(has_down)
    def _():
        greet(me - step_z, core)

    mine_cols = pl.ds(pl.multiple_of(core * share, share), share)
    their_cols = pl.ds(pl.multiple_of(other * share, share), share)
    my_rows = pl.ds(pl.multiple_of(core * half, half), half)
    my_vector_rows = pl.ds(pl.multiple_of(feats + core * half, half), half)
    locals_ = [
        pltpu.make_async_copy(
            points.at[:, mine_cols], blocks.at[me, my_rows, :], local_sem.at[0]),
        pltpu.make_async_copy(
            vectors.at[:, mine_cols], blocks.at[me, my_vector_rows, :], local_sem.at[1]),
        pltpu.make_async_copy(points, own.at[my_rows, :], local_sem.at[2]),
        pltpu.make_async_copy(vectors, mine, local_sem.at[3]),
    ]
    for copy in locals_:
        copy.start()

    neighbours = (1 + 2 * (inner - 1)) + has_up.astype(jnp.int32) + has_down.astype(jnp.int32)
    pl.semaphore_wait(barrier, neighbours)

    pair = [
        remote(points.at[:, their_cols], blocks.at[me, my_rows, :],
               pair_send.at[0], pair_recv.at[0], me, other),
        remote(vectors.at[:, their_cols], blocks.at[me, my_vector_rows, :],
               pair_send.at[1], pair_recv.at[1], me, other),
        remote(points, own.at[my_rows, :], pair_send.at[2], pair_recv.at[2], me, other),
    ]
    for copy in pair:
        copy.start()

    def line_copy(block, direction, zz):
        target = jnp.where(direction == 0, me + step_z, me - step_z)
        return remote(blocks.at[block], blocks.at[block], line_send.at[direction, zz],
                      recv.at[block], target, core)

    def b_copy(block, zz):
        return remote(blocks.at[block], blocks.at[block], b_send.at[zz],
                      recv.at[block], peer_b, core)

    def c_copy(block, slot):
        return remote(blocks.at[block], blocks.at[block], c_send.at[slot],
                      recv.at[block], peer_c, core)

    def line_id(zz, b, c):
        return zz * step_z + (bit_b ^ b) * stride_b + (bit_c ^ c) * stride_c

    order = visit_order(line, inner)
    middle = jnp.minimum(z, line - 1 - z)
    more_up = z < line - 1 - z

    def locate(step):
        rank = pick(step, [item[0] for item in order])
        b = pick(step, [item[1] for item in order])
        c = pick(step, [item[2] for item in order])
        both = rank <= 2 * middle
        distance = jnp.where(both, (rank + 1) // 2, rank - middle)
        upward = jnp.where(both, rank % 2 == 1, more_up)
        zz = jnp.where(upward, z + distance, z - distance)
        return zz, b, c, line_id(zz, b, c)

    def forward(zz, b, c, block):
        @pl.when((b == 0) & (c == 0) & (zz <= z) & has_up)
        def _():
            line_copy(block, 0, zz).start()

        @pl.when((b == 0) & (c == 0) & (zz >= z) & has_down)
        def _():
            line_copy(block, 1, zz).start()

        if inner == 2:
            @pl.when((b == 0) & (c == 0))
            def _():
                b_copy(block, zz).start()

            @pl.when(c == 0)
            def _():
                c_copy(block, zz * 2 + b).start()

    scale = outscale[0]
    top = jnp.log(jnp.full((1, 1), scale, F32)) * LOG2E
    column = jnp.transpose(jnp.broadcast_to(lengths[...], (feats, feats)))[:, 0:1]

    for copy in locals_[:2]:
        copy.wait()
    pair[0].wait_recv()
    pair[1].wait_recv()
    forward(z, jnp.int32(0), jnp.int32(0), me)

    locals_[2].wait()
    pair[2].wait_recv()
    scaled = (own[...].astype(F32) / column).astype(BF16).astype(F32)
    level = -0.5 * LOG2E * jnp.sum(scaled * scaled, axis=0, keepdims=True) + top
    ones = jnp.ones_like(level)
    for index, piece in enumerate(pieces(scaled * LOG2E)):
        own_wide[index * feats:(index + 1) * feats, :] = piece.astype(BF16)
    own_wide[3 * feats:, :] = extra_rows((ones, ones, ones) + pieces(level))
    total[...] = jnp.zeros_like(total)

    def visit(step, carry):
        zz, b, c, block = locate(step)

        @pl.when(step > 0)
        def _():
            c_copy(block, 0).wait_recv()
            forward(zz, b, c, block)

        guest = (blocks[block, 0:feats, :].astype(F32) / column).astype(BF16)
        wide = guest.astype(F32)
        norm = -0.5 * LOG2E * jnp.sum(wide * wide, axis=0, keepdims=True)
        one = jnp.ones_like(norm)
        right = jnp.concatenate(
            [guest, guest, guest, extra_rows(pieces(norm) + (one, one, one))], axis=0)
        power = jnp.dot(right.T, own_wide[...], preferred_element_type=F32)
        value = jnp.exp2(jnp.minimum(power, top)).astype(BF16)
        total[...] += jnp.dot(blocks[block, feats:, :], value, preferred_element_type=F32)
        return carry

    lax.fori_loop(0, len(order), visit, 0)

    other_rows = pl.ds(pl.multiple_of(other * half, half), half)
    part = remote(total.at[other_rows, :], inbox, part_send, part_recv, me, other)
    part.start()
    locals_[3].wait()
    part.wait_recv()
    result[...] = total[my_rows, :] + inbox[...] + noise[0] * mine[...].astype(F32)

    part.wait_send()
    for copy in pair:
        copy.wait_send()

    def drain(zz, carry):
        block = line_id(zz, 0, 0)

        @pl.when((zz <= z) & has_up)
        def _():
            line_copy(block, 0, zz).wait_send()

        @pl.when((zz >= z) & has_down)
        def _():
            line_copy(block, 1, zz).wait_send()

        if inner == 2:
            b_copy(block, zz).wait_send()
            c_copy(block, zz * 2).wait_send()
            c_copy(block, zz * 2 + 1).wait_send()
        return carry

    lax.fori_loop(0, line, drain, 0)


def per_device(blk, points, vectors, lengthscale, outscale, noise):
    inner = 2 if blk % 4 == 0 else 1
    line = blk // (inner * inner)
    rows, half = points.shape
    feats = 2 * half
    share = rows // 2
    vmem = pl.BlockSpec(memory_space=pltpu.VMEM)
    smem = pl.BlockSpec(memory_space=pltpu.SMEM)
    anywhere = pl.BlockSpec(memory_space=pl.ANY)
    dma = pltpu.SemaphoreType.DMA
    out = pl.pallas_call(
        functools.partial(kernel, line, inner),
        out_shape=jax.ShapeDtypeStruct((half, rows), F32),
        in_specs=[anywhere, anywhere, vmem, smem, smem],
        out_specs=vmem,
        scratch_shapes=[
            pltpu.VMEM((blk, 2 * feats, share), BF16),
            pltpu.VMEM((feats, rows), BF16),
            pltpu.VMEM((3 * feats + EXTRA, rows), BF16),
            pltpu.VMEM((feats, rows), F32),
            pltpu.VMEM((half, rows), F32),
            pltpu.VMEM((half, rows), BF16),
            dma((4,)),
            dma((3,)),
            dma((3,)),
            dma((2, line)),
            dma((line,)),
            dma((2 * line,)),
            dma((blk,)),
            dma,
            dma,
        ],
        compiler_params=pltpu.CompilerParams(
            collective_id=0, has_side_effects=True, vmem_limit_bytes=48 << 20
        ),
        name="gather_solve",
    )(points.T, vectors.T, lengthscale.reshape(1, feats), outscale, noise)
    return out.T


def solution(mesh):
    placed = (P("blk", "feat"), P("blk", "feat"), P(), P(), P())
    return jax.shard_map(
        functools.partial(per_device, mesh.shape["blk"]),
        mesh=mesh, in_specs=placed, out_specs=P("blk", "feat"), check_vma=False,
    )
```

time: 163 us -> 42.7 us (0.26)
  waiting for transfers between devices: 113 us -> 0 us
  Pallas kernels: 0 us -> 38.2 us
  matrix products: 19.8 us -> 0 us
  between operations: 13.8 us -> 1.32 us
  local copies, waits for them, and re-layouts: 7.62 us -> 2.98 us
  blocking collectives: 4.15 us -> 0 us
  other arithmetic: 3.93 us -> 0 us
    all_gather x2 -> x0, waiting for transfers between devices: 106 us -> none  [the longest x1 53.2 us: per_device(): lax.all_gather(share_vectors, 'blk', axis=0, tiled=True)]
    pallas_call x0 -> x1, Pallas kernels: none -> 38.2 us  [per_device(): pl.pallas_call(functools.partial(kernel, line, inner), out_shape=jax.Shap...]
    dot_general x4 -> x0, matrix products: 19.8 us -> none  [advance(): jnp.dot(kernel_block, group_vectors, preferred_element_type=jnp.float32)]
    reduce_scatter x1 -> x0, waiting for transfers between devices: 6.58 us -> none  [per_device(): result = lax.psum_scatter(direct, 'feat', scatter_dimension=1, tiled=True)]
    all_gather x2 -> x0, blocking collectives: 4.15 us -> none  [the longest x1 2.11 us: per_device(): lax.all_gather(vectors, 'feat', axis=1, tiled=True)]
    all_gather x1 -> x0, local copies, waits for them, and re-layouts: 2.76 us -> none  [per_device(): lax.all_gather(share_vectors, 'blk', axis=0, tiled=True)]
    dynamic_slice x3 -> x0, local copies, waits for them, and re-layouts: 1.98 us -> none  [the longest x1 0.73 us: per_device(): lax.dynamic_slice_in_dim(lengthscale, feat_index * feature_width, feature...]
  transfers between devices with their start and end apart: 3 -> 0, of which waited for: 3 -> 0; matrix products, arithmetic and copies ran while one was open for 2% -> 0% of each run, Pallas kernels for 0% -> 0%
where the time goes in v1:
time: 42.7 us; the launch traced here: 42.5 us
  Pallas kernels  38.2 us (89%)
  local copies, waits for them, and re-layouts  2.98 us (7%)
  between operations  1.32 us (3%)
    pallas_call x1, Pallas kernels, per_device(): pl.pallas_call(functools.partial(kernel, line, inner), out_shape=jax.Shap...  38.2 us
    unnamed x7, local copies, waits for them, and re-layouts  2.98 us

profile of v1, /device:TPU:0, one launch (start us, length us, event | category | flops | bytes accessed | tf_op | source)
XLA Modules:
  0.0 42.5 jit_solution(15805198236270837588)
XLA Ops:
  1.3 0.0 copy-start.2
  1.3 0.6 %copy-done.2 = f32[64]{0:T(128)S(1)} copy-done((f32[64]{0:T(128)S(1)}, f32[64]{0:T(128)}, u32[]{:S(2)}) %copy-start.2) | copy-done | bytes 280
  2.0 0.0 copy-start
  2.0 0.8 %copy-done = bf16[1024,32]{0,1:T(8,128)(2,1)S(1)} copy-done((bf16[1024,32]{0,1:T(8,128)(2,1)S(1)}, bf16[1024,32]{0,1:T(8,128)(2,1)}, u32[]{:S(2)}) %copy-start) | copy-done | bytes 65560
  2.8 0.0 copy-start.1
  2.8 0.8 %copy-done.1 = bf16[1024,32]{0,1:T(8,128)(2,1)S(1)} copy-done((bf16[1024,32]{0,1:T(8,128)(2,1)S(1)}, bf16[1024,32]{0,1:T(8,128)(2,1)}, u32[]{:S(2)}) %copy-start.1) | copy-done | bytes 65560
  3.6 38.2 %gather_solve.1 = f32[32,1024]{1,0:T(8,128)S(1)} custom-call(bf16[32,1024]{1,0:T(8,128)(2,1)S(1)} %bitcast.5, bf16[32,1024]{1,0:T(8,128)(2,1)S(1)} %bitcast.6, f32[1,64]{1,0:T(1,128)S(1)} %bitcast.7, f32[1]{0:T(128)S(6)} %copy.7.outscale, f32[1]{0:T(128)S(6)} %copy.8.noise), custom_call_target="tpu_custom_call" | custom-call | tf_op jit(solution)/shard_map/gather_solve/pallas_call | solution.py:266
  41.8 0.7 %copy.9 = f32[1024,32]{0,1:T(8,128)} copy(f32[1024,32]{0,1:T(8,128)S(1)} %bitcast.4) | data formatting | bytes 262144
Async XLA Ops:
  1.3 0.7 %copy-start.2 = (f32[64]{0:T(128)S(1)}, f32[64]{0:T(128)}, u32[]{:S(2)}) copy-start(f32[64]{0:T(128)} %param.7) | copy-start | bytes 772
  2.0 0.8 %copy-start = (bf16[1024,32]{0,1:T(8,128)(2,1)S(1)}, bf16[1024,32]{0,1:T(8,128)(2,1)}, u32[]{:S(2)}) copy-start(bf16[1024,32]{0,1:T(8,128)(2,1)} %param.5) | copy-start | bytes 196612
  2.8 0.8 %copy-start.1 = (bf16[1024,32]{0,1:T(8,128)(2,1)S(1)}, bf16[1024,32]{0,1:T(8,128)(2,1)}, u32[]{:S(2)}) copy-start(bf16[1024,32]{0,1:T(8,128)(2,1)} %param.6) | copy-start | bytes 196612

commit v2 on v0

v2 whole, which is shorter than its diff:
```python
import functools

import jax
import jax.numpy as jnp
from jax import lax
from jax.experimental import pallas as pl
from jax.experimental.pallas import tpu as pltpu
from jax.sharding import PartitionSpec as P

LOG2E = 1.4426950408889634
F32 = jnp.float32
BF16 = jnp.bfloat16
EXTRA = 16
SIDE = 2
PLANE = SIDE * SIDE


def pieces(value):
    first = value.astype(BF16).astype(F32)
    rest = value - first
    second = rest.astype(BF16).astype(F32)
    return first, second, rest - second


def extra_rows(rows):
    shape = (EXTRA, rows[0].shape[1])
    place = lax.broadcasted_iota(jnp.int32, shape, 0)
    out = jnp.zeros(shape, F32)
    for index, row in enumerate(rows):
        out = jnp.where(place == index, row, out)
    return out.astype(BF16)


def kernel(
    line, points, vectors, lengths, outscale, noise, result,
    columns, row_points, right, left, total, inbox, mine, swap_out, swap_in,
    local_sem, pair_send, pair_recv, plane_send, plane_recv, twin_send, twin_recv,
    row_send, row_recv, part_send, part_recv, swap_send, swap_recv,
):
    me = lax.axis_index("blk")
    core = lax.axis_index("feat")
    other = 1 - core
    half, rows = points.shape
    feats = 2 * half
    share = rows // 2
    z = me // PLANE
    spot = me % PLANE

    def remote(src, dst, send, arrive, blk, feat):
        return pltpu.make_async_remote_copy(
            src_ref=src, dst_ref=dst, send_sem=send, recv_sem=arrive,
            device_id={"blk": blk, "feat": feat}, device_id_type=pl.DeviceIdType.MESH,
        )

    barrier = pltpu.get_barrier_semaphore()

    def greet(blk, feat):
        pl.semaphore_signal(
            barrier, inc=1, device_id={"blk": blk, "feat": feat},
            device_id_type=pl.DeviceIdType.MESH,
        )

    def plane_peer(index):
        return z * PLANE + (spot ^ index)

    def line_peer(step):
        return lax.rem(z + step, line) * PLANE + spot

    greet(me, other)
    for index in range(1, PLANE):
        greet(plane_peer(index), core)
    for step in range(1, line):
        greet(line_peer(step), core)

    my_rows = pl.ds(pl.multiple_of(core * half, half), half)
    my_vector_rows = pl.ds(pl.multiple_of(feats + core * half, half), half)

    locals_ = []
    pair = []
    for part in range(2):
        cols = pl.ds(part * share, share)
        for place, (array, spot_rows) in enumerate(((points, my_rows), (vectors, my_vector_rows))):
            slot = 2 * part + place
            target = columns.at[0, part, spot_rows, :]
            locals_.append(
                pltpu.make_async_copy(array.at[:, cols], target, local_sem.at[slot]))
            pair.append(
                remote(array.at[:, cols], target, pair_send.at[slot], pair_recv.at[slot],
                       me, other))
    locals_.append(pltpu.make_async_copy(vectors, mine, local_sem.at[4]))
    for copy in locals_:
        copy.start()
    pl.semaphore_wait(barrier, PLANE + line - 1)
    for copy in pair:
        copy.start()

    scale = outscale[0]
    top = jnp.log(jnp.full((1, 1), scale, F32)) * LOG2E
    column = jnp.transpose(jnp.broadcast_to(lengths[...], (feats, feats)))[:, 0:1]

    for copy in locals_:
        copy.wait()
    for copy in pair:
        copy.wait_recv()

    plane = []
    for index in range(1, PLANE):
        plane.append(
            remote(columns.at[0, core], columns.at[index, core], plane_send.at[index],
                   plane_recv.at[index], plane_peer(index), core))
    spread = []
    for step in range(1, line):
        spread.append(
            remote(columns.at[0, core, 0:feats, :], row_points.at[line - step],
                   row_send.at[step], row_recv.at[line - step], line_peer(step), core))
    near_first = []
    for place in range(max(len(plane), len(spread))):
        near_first += plane[place:place + 1] + spread[place:place + 1]
    for copy in near_first:
        copy.start()

    def twin(index):
        return remote(columns.at[index, core], columns.at[index, core], twin_send.at[index],
                      twin_recv.at[index], me, other)

    def other_twin(index):
        return remote(columns.at[index, other], columns.at[index, other], twin_send.at[index],
                      twin_recv.at[index], me, other)

    def fetch(index):
        plane[index - 1].wait_recv()
        twin(index).start()

    def prepare_columns(index):
        if index > 0:
            other_twin(index).wait_recv()
        for part in range(2):
            guest = (columns[index, part, 0:feats, :].astype(F32) / column).astype(BF16)
            wide = guest.astype(F32)
            norm = -0.5 * LOG2E * jnp.sum(wide * wide, axis=0, keepdims=True)
            one = jnp.ones_like(norm)
            stacked = jnp.concatenate(
                [guest, guest, guest, extra_rows(pieces(norm) + (one, one, one))], axis=0)
            right[index, part * share:(part + 1) * share, :] = stacked.T

    def prepare_rows(value):
        scaled = (value.astype(F32) / column).astype(BF16).astype(F32)
        level = -0.5 * LOG2E * jnp.sum(scaled * scaled, axis=0, keepdims=True) + top
        one = jnp.ones_like(level)
        for index, piece in enumerate(pieces(scaled * LOG2E)):
            left[index * feats:(index + 1) * feats, :] = piece.astype(BF16)
        left[3 * feats:, :] = extra_rows((one, one, one) + pieces(level))

    def unit(slot, index, start):
        power = jnp.dot(right[index], left[...], preferred_element_type=F32)
        value = jnp.exp2(jnp.minimum(power, top)).astype(BF16)
        acc = jnp.dot(columns[index, 0, feats:, :], value[0:share], preferred_element_type=F32)
        acc += jnp.dot(columns[index, 1, feats:, :], value[share:], preferred_element_type=F32)
        if start:
            total[slot] = acc
        else:
            total[slot] += acc

    def give_back(step):
        return remote(total.at[step], inbox.at[line - step], part_send.at[step],
                      part_recv.at[line - step], line_peer(step), core)

    prepare_columns(0)
    prepare_rows(columns[0, core, 0:feats, :])
    unit(0, 0, True)
    fetch(1)

    def one_row(step, carry):
        row_copy = remote(columns.at[0, core, 0:feats, :], row_points.at[step],
                          row_send.at[step], row_recv.at[step], line_peer(step), core)
        row_copy.wait_recv()
        prepare_rows(row_points[step])
        for index in range(PLANE):
            if index > 0:
                @pl.when(step == 1)
                def _():
                    if index + 1 < PLANE:
                        fetch(index + 1)
                    prepare_columns(index)

            unit(step, index, index == 0)
            if index == 0:
                @pl.when(step > 1)
                def _():
                    give_back(step - 1).start()
        return carry

    lax.fori_loop(1, line, one_row, 0)

    prepare_rows(columns[0, core, 0:feats, :])
    for index in range(1, PLANE):
        unit(0, index, False)
        if index == 1:
            give_back(line - 1).start()

    def collect(step, carry):
        give_back(line - step).wait_recv()
        total[0] += inbox[step]
        return carry

    lax.fori_loop(1, line, collect, 0)

    other_rows = pl.ds(pl.multiple_of(other * half, half), half)
    swap_out[...] = total[0, other_rows, :]
    swap = remote(swap_out, swap_in, swap_send, swap_recv, me, other)
    factor = noise[0]
    my_cols = pl.ds(pl.multiple_of(core * share, share), share)
    other_cols = pl.ds(pl.multiple_of(other * share, share), share)
    result[:, my_cols] = total[0, my_rows, :] + factor * mine[:, my_cols].astype(F32)
    swap.start()
    swap.wait_recv()
    result[:, other_cols] = swap_in[...] + factor * mine[:, other_cols].astype(F32)

    swap.wait_send()
    for copy in pair + plane + spread:
        copy.wait_send()
    for index in range(1, PLANE):
        twin(index).wait_send()

    def drain(step, carry):
        give_back(step).wait_send()
        return carry

    lax.fori_loop(1, line, drain, 0)


def per_device(blk, points, vectors, lengthscale, outscale, noise):
    assert blk % PLANE == 0 and blk > PLANE
    line = blk // PLANE
    rows, half = points.shape
    feats = 2 * half
    share = rows // 2
    vmem = pl.BlockSpec(memory_space=pltpu.VMEM)
    smem = pl.BlockSpec(memory_space=pltpu.SMEM)
    anywhere = pl.BlockSpec(memory_space=pl.ANY)
    dma = pltpu.SemaphoreType.DMA
    wide = 3 * feats + EXTRA
    out = pl.pallas_call(
        functools.partial(kernel, line),
        out_shape=jax.ShapeDtypeStruct((half, rows), F32),
        in_specs=[anywhere, anywhere, vmem, smem, smem],
        out_specs=vmem,
        scratch_shapes=[
            pltpu.VMEM((PLANE, 2, 2 * feats, share), BF16),
            pltpu.VMEM((line, feats, share), BF16),
            pltpu.VMEM((PLANE, rows, wide), BF16),
            pltpu.VMEM((wide, share), BF16),
            pltpu.VMEM((line, feats, share), F32),
            pltpu.VMEM((line, feats, share), F32),
            pltpu.VMEM((half, rows), BF16),
            pltpu.VMEM((half, share), F32),
            pltpu.VMEM((half, share), F32),
            dma((5,)),
            dma((4,)),
            dma((4,)),
            dma((PLANE,)),
            dma((PLANE,)),
            dma((PLANE,)),
            dma((PLANE,)),
            dma((line,)),
            dma((line,)),
            dma((line,)),
            dma((line,)),
            dma,
            dma,
        ],
        compiler_params=pltpu.CompilerParams(collective_id=0, has_side_effects=True),
        name="plane_line_solve",
    )(points.T, vectors.T, lengthscale.reshape(1, feats), outscale, noise)
    return out.T


def solution(mesh):
    placed = (P("blk", "feat"), P("blk", "feat"), P(), P(), P())
    return jax.shard_map(
        functools.partial(per_device, mesh.shape["blk"]),
        mesh=mesh, in_specs=placed, out_specs=P("blk", "feat"), check_vma=False,
    )
```

time: 163 us -> 36.2 us (0.22)
  waiting for transfers between devices: 113 us -> 0 us
  Pallas kernels: 0 us -> 33.2 us
  matrix products: 19.8 us -> 0 us
  between operations: 13.8 us -> 1.3 us
  local copies, waits for them, and re-layouts: 7.62 us -> 1.57 us
  blocking collectives: 4.15 us -> 0 us
  other arithmetic: 3.93 us -> 0 us
    all_gather x2 -> x0, waiting for transfers between devices: 106 us -> none  [the longest x1 53.2 us: per_device(): lax.all_gather(share_vectors, 'blk', axis=0, tiled=True)]
    pallas_call x0 -> x1, Pallas kernels: none -> 33.2 us  [per_device(): pl.pallas_call(functools.partial(kernel, line), out_shape=jax.ShapeDtypeS...]
    dot_general x4 -> x0, matrix products: 19.8 us -> none  [advance(): jnp.dot(kernel_block, group_vectors, preferred_element_type=jnp.float32)]
    reduce_scatter x1 -> x0, waiting for transfers between devices: 6.58 us -> none  [per_device(): result = lax.psum_scatter(direct, 'feat', scatter_dimension=1, tiled=True)]
    all_gather x2 -> x0, blocking collectives: 4.15 us -> none  [the longest x1 2.11 us: per_device(): lax.all_gather(vectors, 'feat', axis=1, tiled=True)]
    all_gather x1 -> x0, local copies, waits for them, and re-layouts: 2.76 us -> none  [per_device(): lax.all_gather(share_vectors, 'blk', axis=0, tiled=True)]
    dynamic_slice x3 -> x0, local copies, waits for them, and re-layouts: 1.98 us -> none  [the longest x1 0.73 us: per_device(): lax.dynamic_slice_in_dim(lengthscale, feat_index * feature_width, feature...]
  transfers between devices with their start and end apart: 3 -> 0, of which waited for: 3 -> 0; matrix products, arithmetic and copies ran while one was open for 2% -> 0% of each run, Pallas kernels for 0% -> 0%
where the time goes in v2:
time: 36.2 us; the launch traced here: 36 us
  Pallas kernels  33.2 us (92%)
  local copies, waits for them, and re-layouts  1.57 us (4%)
  between operations  1.3 us (4%)
    pallas_call x1, Pallas kernels, per_device(): pl.pallas_call(functools.partial(kernel, line), out_shape=jax.ShapeDtypeS...  33.2 us
    unnamed x1, local copies, waits for them, and re-layouts  1.57 us

profile of v2, /device:TPU:0, one launch (start us, length us, event | category | flops | bytes accessed | tf_op | source)
XLA Modules:
  0.0 36.0 jit_solution(802474937630793908)
XLA Ops:
  1.3 33.2 %plane_line_solve.1 = f32[32,1024]{1,0:T(8,128)} custom-call(bf16[32,1024]{1,0:T(8,128)(2,1)} %bitcast.5, bf16[32,1024]{1,0:T(8,128)(2,1)} %bitcast.6, f32[1,64]{1,0:T(1,128)} %bitcast.7, f32[1]{0:T(128)S(6)} %copy.7.outscale, f32[1]{0:T(128)S(6)} %copy.8.noise), custom_call_target="tpu_custom_call" | custom-call | tf_op jit(solution)/shard_map/plane_line_solve/pallas_call | solution.py:243
  34.5 1.6 %copy.9 = f32[1024,32]{0,1:T(8,128)} copy(f32[1024,32]{0,1:T(8,128)} %bitcast.4) | data formatting | bytes 262144

commit v3 on v2

--- a/solution.py
+++ b/solution.py
@@ -11,8 +11,7 @@
 F32 = jnp.float32
 BF16 = jnp.bfloat16
 EXTRA = 16
-SIDE = 2
-PLANE = SIDE * SIDE
+PLANE = 4
 
 
 def pieces(value):
@@ -43,8 +42,6 @@
     half, rows = points.shape
     feats = 2 * half
     share = rows // 2
-    z = me // PLANE
-    spot = me % PLANE
 
     def remote(src, dst, send, arrive, blk, feat):
         return pltpu.make_async_remote_copy(
@@ -60,17 +57,17 @@
             device_id_type=pl.DeviceIdType.MESH,
         )
 
-    def plane_peer(index):
-        return z * PLANE + (spot ^ index)
-
-    def line_peer(step):
-        return lax.rem(z + step, line) * PLANE + spot
+    def column_peer(index):
+        return me ^ ((index % 2) * 2 + (index // 2) * (2 * line))
+
+    def row_peer(step):
+        return me ^ (step % 2 + (step // 2) * PLANE)
 
     greet(me, other)
-    for index in range(1, PLANE):
-        greet(plane_peer(index), core)
+    greet(column_peer(1), core)
+    greet(column_peer(2), core)
     for step in range(1, line):
-        greet(line_peer(step), core)
+        greet(row_peer(step), core)
 
     my_rows = pl.ds(pl.multiple_of(core * half, half), half)
     my_vector_rows = pl.ds(pl.multiple_of(feats + core * half, half), half)
@@ -90,7 +87,7 @@
     locals_.append(pltpu.make_async_copy(vectors, mine, local_sem.at[4]))
     for copy in locals_:
         copy.start()
-    pl.semaphore_wait(barrier, PLANE + line - 1)
+    pl.semaphore_wait(barrier, 2 + line)
     for copy in pair:
         copy.start()
 
@@ -103,21 +100,22 @@
     for copy in pair:
         copy.wait_recv()
 
-    plane = []
-    for index in range(1, PLANE):
-        plane.append(
-            remote(columns.at[0, core], columns.at[index, core], plane_send.at[index],
-                   plane_recv.at[index], plane_peer(index), core))
-    spread = []
-    for step in range(1, line):
-        spread.append(
-            remote(columns.at[0, core, 0:feats, :], row_points.at[line - step],
-                   row_send.at[step], row_recv.at[line - step], line_peer(step), core))
-    near_first = []
-    for place in range(max(len(plane), len(spread))):
-        near_first += plane[place:place + 1] + spread[place:place + 1]
-    for copy in near_first:
-        copy.start()
+    def row_copy(step):
+        return remote(columns.at[0, core, 0:feats, :], row_points.at[step],
+                      row_send.at[step], row_recv.at[step], row_peer(step), core)
+
+    def column_copy(index):
+        source = 0 if index < 3 else 2
+        return remote(columns.at[source, core], columns.at[index, core], plane_send.at[index],
+                      plane_recv.at[index], column_peer(1 if index == 3 else index), core)
+
+    def start_row(step, carry):
+        row_copy(step).start()
+        return carry
+
+    lax.fori_loop(1, line, start_row, 0)
+    column_copy(1).start()
+    column_copy(2).start()
 
     def twin(index):
         return remote(columns.at[index, core], columns.at[index, core], twin_send.at[index],
@@ -128,7 +126,9 @@
                       twin_recv.at[index], me, other)
 
     def fetch(index):
-        plane[index - 1].wait_recv()
+        column_copy(index).wait_recv()
+        if index == 2:
+            column_copy(3).start()
         twin(index).start()
 
     def prepare_columns(index):
@@ -143,67 +143,77 @@
                 [guest, guest, guest, extra_rows(pieces(norm) + (one, one, one))], axis=0)
             right[index, part * share:(part + 1) * share, :] = stacked.T
 
-    def prepare_rows(value):
+    def prepare_rows(step, value):
         scaled = (value.astype(F32) / column).astype(BF16).astype(F32)
         level = -0.5 * LOG2E * jnp.sum(scaled * scaled, axis=0, keepdims=True) + top
         one = jnp.ones_like(level)
         for index, piece in enumerate(pieces(scaled * LOG2E)):
-            left[index * feats:(index + 1) * feats, :] = piece.astype(BF16)
-        left[3 * feats:, :] = extra_rows((one, one, one) + pieces(level))
-
-    def unit(slot, index, start):
-        power = jnp.dot(right[index], left[...], preferred_element_type=F32)
+            left[step, index * feats:(index + 1) * feats, :] = piece.astype(BF16)
+        left[step, 3 * feats:, :] = extra_rows((one, one, one) + pieces(level))
+
+    def unit(step, index, parts=(0, 1)):
+        guests = slice(parts[0] * share, (parts[-1] + 1) * share)
+        power = jnp.dot(right[index, guests, :], left[step], preferred_element_type=F32)
         value = jnp.exp2(jnp.minimum(power, top)).astype(BF16)
-        acc = jnp.dot(columns[index, 0, feats:, :], value[0:share], preferred_element_type=F32)
-        acc += jnp.dot(columns[index, 1, feats:, :], value[share:], preferred_element_type=F32)
-        if start:
-            total[slot] = acc
-        else:
-            total[slot] += acc
+        for place, part in enumerate(parts):
+            total[step] += jnp.dot(
+                columns[index, part, feats:, :], value[place * share:(place + 1) * share],
+                preferred_element_type=F32)
 
     def give_back(step):
-        return remote(total.at[step], inbox.at[line - step], part_send.at[step],
-                      part_recv.at[line - step], line_peer(step), core)
-
+        return remote(total.at[step], inbox.at[step], part_send.at[step],
+                      part_recv.at[step], row_peer(step), core)
+
+    total[...] = jnp.zeros_like(total)
     prepare_columns(0)
-    prepare_rows(columns[0, core, 0:feats, :])
-    unit(0, 0, True)
-    fetch(1)
-
-    def one_row(step, carry):
-        row_copy = remote(columns.at[0, core, 0:feats, :], row_points.at[step],
-                          row_send.at[step], row_recv.at[step], line_peer(step), core)
-        row_copy.wait_recv()
-        prepare_rows(row_points[step])
-        for index in range(PLANE):
-            if index > 0:
-                @pl.when(step == 1)
+    for index in range(PLANE - 1):
+        if index > 0:
+            prepare_columns(index)
+
+        def one_row(step, carry):
+            if index == 0:
+                @pl.when(step == 0)
                 def _():
-                    if index + 1 < PLANE:
-                        fetch(index + 1)
-                    prepare_columns(index)
-
-            unit(step, index, index == 0)
-            if index == 0:
-                @pl.when(step > 1)
+                    prepare_rows(step, columns[0, core, 0:feats, :])
+
+                @pl.when(step > 0)
                 def _():
-                    give_back(step - 1).start()
-        return carry
-
-    lax.fori_loop(1, line, one_row, 0)
-
-    prepare_rows(columns[0, core, 0:feats, :])
-    for index in range(1, PLANE):
-        unit(0, index, False)
-        if index == 1:
-            give_back(line - 1).start()
-
-    def collect(step, carry):
-        give_back(line - step).wait_recv()
+                    row_copy(step).wait_recv()
+                    prepare_rows(step, row_points[step])
+
+            @pl.when(step == line - 2)
+            def _():
+                fetch(index + 1)
+
+            unit(step, index)
+            return carry
+
+        lax.fori_loop(0, line, one_row, 0)
+
+    last = PLANE - 1
+    prepare_columns(last)
+
+    def last_row(place, carry):
+        step = line - 1 - place
+        unit(step, last)
+
+        @pl.when(place > 0)
+        def _():
+            give_back(step + 1).start()
+        return carry
+
+    lax.fori_loop(0, line - 1, last_row, 0)
+    unit(0, last, (0,))
+    give_back(1).start()
+    unit(0, last, (1,))
+
+    def collect(place, carry):
+        step = line - 1 - place
+        give_back(step).wait_recv()
         total[0] += inbox[step]
         return carry
 
-    lax.fori_loop(1, line, collect, 0)
+    lax.fori_loop(0, line - 1, collect, 0)
 
     other_rows = pl.ds(pl.multiple_of(other * half, half), half)
     swap_out[...] = total[0, other_rows, :]
@@ -217,20 +227,22 @@
     result[:, other_cols] = swap_in[...] + factor * mine[:, other_cols].astype(F32)
 
     swap.wait_send()
-    for copy in pair + plane + spread:
+    for copy in pair:
         copy.wait_send()
     for index in range(1, PLANE):
+        column_copy(index).wait_send()
         twin(index).wait_send()
 
     def drain(step, carry):
         give_back(step).wait_send()
+        row_copy(step).wait_send()
         return carry
 
     lax.fori_loop(1, line, drain, 0)
 
 
 def per_device(blk, points, vectors, lengthscale, outscale, noise):
-    assert blk % PLANE == 0 and blk > PLANE
+    assert blk % (2 * PLANE) == 0 and blk & (blk - 1) == 0
     line = blk // PLANE
     rows, half = points.shape
     feats = 2 * half
@@ -249,7 +261,7 @@
             pltpu.VMEM((PLANE, 2, 2 * feats, share), BF16),
             pltpu.VMEM((line, feats, share), BF16),
             pltpu.VMEM((PLANE, rows, wide), BF16),
-            pltpu.VMEM((wide, share), BF16),
+            pltpu.VMEM((line, wide, share), BF16),
             pltpu.VMEM((line, feats, share), F32),
             pltpu.VMEM((line, feats, share), F32),
             pltpu.VMEM((half, rows), BF16),
@@ -270,7 +282,7 @@
             dma,
         ],
         compiler_params=pltpu.CompilerParams(collective_id=0, has_side_effects=True),
-        name="plane_line_solve",
+        name="tile_solve",
     )(points.T, vectors.T, lengthscale.reshape(1, feats), outscale, noise)
     return out.T
 

time: 36.2 us -> 36.1 us (level); the launches traced: 36 us -> 35.4 us
  Pallas kernels: 33.2 us -> 32.5 us
    pallas_call x1, Pallas kernels: 33.2 us -> 32.5 us  [per_device(): pl.pallas_call(functools.partial(kernel, line), out_shape=jax.ShapeDtypeS...]
where the time goes in v3:
time: 36.1 us; the launch traced here: 35.4 us
  Pallas kernels  32.5 us (90%)
  local copies, waits for them, and re-layouts  1.57 us (4%)
  between operations  1.3 us (4%)
    pallas_call x1, Pallas kernels, per_device(): pl.pallas_call(functools.partial(kernel, line), out_shape=jax.ShapeDtypeS...  32.5 us
    unnamed x1, local copies, waits for them, and re-layouts  1.57 us

profile of v3, /device:TPU:0, one launch (start us, length us, event | category | flops | bytes accessed | tf_op | source)
XLA Modules:
  0.0 35.4 jit_solution(4763629608309455662)
XLA Ops:
  1.3 32.5 %tile_solve.1 = f32[32,1024]{1,0:T(8,128)} custom-call(bf16[32,1024]{1,0:T(8,128)(2,1)} %bitcast.5, bf16[32,1024]{1,0:T(8,128)(2,1)} %bitcast.6, f32[1,64]{1,0:T(1,128)} %bitcast.7, f32[1]{0:T(128)S(6)} %copy.7.outscale, f32[1]{0:T(128)S(6)} %copy.8.noise), custom_call_target="tpu_custom_call" | custom-call | tf_op jit(solution)/shard_map/tile_solve/pallas_call | solution.py:255
  33.8 1.6 %copy.9 = f32[1024,32]{0,1:T(8,128)} copy(f32[1024,32]{0,1:T(8,128)} %bitcast.4) | data formatting | bytes 262144

commit v4 on v3

--- a/solution.py
+++ b/solution.py
@@ -31,7 +31,8 @@
 
 
 def kernel(
-    line, points, vectors, lengths, outscale, noise, result,
+    line, points, vectors, lengths_in, outscale_in, noise_in, result,
+    lengths, outscale, noise, small_sem,
     columns, row_points, right, left, total, inbox, mine, swap_out, swap_in,
     local_sem, pair_send, pair_recv, plane_send, plane_recv, twin_send, twin_recv,
     row_send, row_recv, part_send, part_recv, swap_send, swap_recv,
@@ -49,6 +50,13 @@
             device_id={"blk": blk, "feat": feat}, device_id_type=pl.DeviceIdType.MESH,
         )
 
+    small = [
+        pltpu.make_async_copy(lengths_in, lengths, small_sem.at[0]),
+        pltpu.make_async_copy(outscale_in, outscale, small_sem.at[1]),
+        pltpu.make_async_copy(noise_in, noise, small_sem.at[2]),
+    ]
+    for copy in small:
+        copy.start()
     barrier = pltpu.get_barrier_semaphore()
 
     def greet(blk, feat):
@@ -91,6 +99,8 @@
     for copy in pair:
         copy.start()
 
+    for copy in small:
+        copy.wait()
     scale = outscale[0]
     top = jnp.log(jnp.full((1, 1), scale, F32)) * LOG2E
     column = jnp.transpose(jnp.broadcast_to(lengths[...], (feats, feats)))[:, 0:1]
@@ -104,36 +114,38 @@
         return remote(columns.at[0, core, 0:feats, :], row_points.at[step],
                       row_send.at[step], row_recv.at[step], row_peer(step), core)
 
-    def column_copy(index):
+    def part_of(index, owner, piece):
+        return columns.at[index, owner, pl.ds(piece * feats, feats), :]
+
+    def column_copy(index, piece):
         source = 0 if index < 3 else 2
-        return remote(columns.at[source, core], columns.at[index, core], plane_send.at[index],
-                      plane_recv.at[index], column_peer(1 if index == 3 else index), core)
+        return remote(part_of(source, core, piece), part_of(index, core, piece),
+                      plane_send.at[index, piece], plane_recv.at[index, piece],
+                      column_peer(1 if index == 3 else index), core)
 
     def start_row(step, carry):
         row_copy(step).start()
         return carry
 
     lax.fori_loop(1, line, start_row, 0)
-    column_copy(1).start()
-    column_copy(2).start()
-
-    def twin(index):
-        return remote(columns.at[index, core], columns.at[index, core], twin_send.at[index],
-                      twin_recv.at[index], me, other)
-
-    def other_twin(index):
-        return remote(columns.at[index, other], columns.at[index, other], twin_send.at[index],
-                      twin_recv.at[index], me, other)
-
-    def fetch(index):
-        column_copy(index).wait_recv()
+    for piece in range(2):
+        column_copy(1, piece).start()
+        column_copy(2, piece).start()
+
+    def twin(index, owner, piece):
+        return remote(part_of(index, owner, piece), part_of(index, owner, piece),
+                      twin_send.at[index, piece], twin_recv.at[index, piece], me, other)
+
+    def fetch(index, piece):
+        column_copy(index, piece).wait_recv()
         if index == 2:
-            column_copy(3).start()
-        twin(index).start()
+            column_copy(3, piece).start()
+        twin(index, core, piece).start()
 
     def prepare_columns(index):
         if index > 0:
-            other_twin(index).wait_recv()
+            for piece in range(2):
+                twin(index, other, piece).wait_recv()
         for part in range(2):
             guest = (columns[index, part, 0:feats, :].astype(F32) / column).astype(BF16)
             wide = guest.astype(F32)
@@ -183,7 +195,14 @@
 
             @pl.when(step == line - 2)
             def _():
-                fetch(index + 1)
+                if index == 0:
+                    fetch(1, 0)
+                fetch(index + 1, 1)
+
+            if index < PLANE - 2:
+                @pl.when(step == line - 1)
+                def _():
+                    fetch(index + 2, 0)
 
             unit(step, index)
             return carry
@@ -230,8 +249,9 @@
     for copy in pair:
         copy.wait_send()
     for index in range(1, PLANE):
-        column_copy(index).wait_send()
-        twin(index).wait_send()
+        for piece in range(2):
+            column_copy(index, piece).wait_send()
+            twin(index, core, piece).wait_send()
 
     def drain(step, carry):
         give_back(step).wait_send()
@@ -248,16 +268,19 @@
     feats = 2 * half
     share = rows // 2
     vmem = pl.BlockSpec(memory_space=pltpu.VMEM)
-    smem = pl.BlockSpec(memory_space=pltpu.SMEM)
-    anywhere = pl.BlockSpec(memory_space=pl.ANY)
+    stay = pl.BlockSpec(memory_space=pltpu.HBM)
     dma = pltpu.SemaphoreType.DMA
     wide = 3 * feats + EXTRA
     out = pl.pallas_call(
         functools.partial(kernel, line),
         out_shape=jax.ShapeDtypeStruct((half, rows), F32),
-        in_specs=[anywhere, anywhere, vmem, smem, smem],
+        in_specs=[stay] * 5,
         out_specs=vmem,
         scratch_shapes=[
+            pltpu.VMEM((1, feats), F32),
+            pltpu.SMEM((1,), F32),
+            pltpu.SMEM((1,), F32),
+            dma((3,)),
             pltpu.VMEM((PLANE, 2, 2 * feats, share), BF16),
             pltpu.VMEM((line, feats, share), BF16),
             pltpu.VMEM((PLANE, rows, wide), BF16),
@@ -270,10 +293,10 @@
             dma((5,)),
             dma((4,)),
             dma((4,)),
-            dma((PLANE,)),
-            dma((PLANE,)),
-            dma((PLANE,)),
-            dma((PLANE,)),
+            dma((PLANE, 2)),
+            dma((PLANE, 2)),
+            dma((PLANE, 2)),
+            dma((PLANE, 2)),
             dma((line,)),
             dma((line,)),
             dma((line,)),

time: 36.1 us -> 34.1 us (0.945); the launches traced: 35.4 us -> 33.9 us
  Pallas kernels: 32.5 us -> 31 us
    pallas_call x1, Pallas kernels: 32.5 us -> 31 us  [per_device(): pl.pallas_call(functools.partial(kernel, line), out_shape=jax.ShapeDtypeS...]
where the time goes in v4:
time: 34.1 us; the launch traced here: 33.9 us
  Pallas kernels  31 us (91%)
  local copies, waits for them, and re-layouts  1.57 us (5%)
  between operations  1.3 us (4%)
    pallas_call x1, Pallas kernels, per_device(): pl.pallas_call(functools.partial(kernel, line), out_shape=jax.ShapeDtypeS...  31 us
    unnamed x1, local copies, waits for them, and re-layouts  1.57 us

profile of v4, /device:TPU:0, one launch (start us, length us, event | category | flops | bytes accessed | tf_op | source)
XLA Modules:
  0.0 33.9 jit_solution(2064324025848743365)
XLA Ops:
  1.3 31.0 %tile_solve.1 = f32[32,1024]{1,0:T(8,128)} custom-call(bf16[32,1024]{1,0:T(8,128)(2,1)} %bitcast.5, bf16[32,1024]{1,0:T(8,128)(2,1)} %bitcast.6, f32[1,64]{1,0:T(1,128)} %bitcast.7, f32[1]{0:T(128)S(6)} %copy.7.outscale_in, f32[1]{0:T(128)S(6)} %copy.8.noise_in), custom_call_target="tpu_custom_call" | custom-call | tf_op jit(solution)/shard_map/tile_solve/pallas_call | solution.py:274
  32.3 1.6 %copy.9 = f32[1024,32]{0,1:T(8,128)} copy(f32[1024,32]{0,1:T(8,128)} %bitcast.4) | data formatting | bytes 262144
